TPU v7x, 256 devices: a whole 4x4x8 slice. The times are simulated.
256 devices in a mesh: dp: 32 (over y, z), tensor: 8 (over x, core).
Axes of the slice: x: 4, y: 4, z: 8, core: 2. Of those that a mesh axis runs over, the one named last changes fastest.
Arguments:
- queries: bfloat16 [256, 6, 8192], P('dp', None, 'tensor'), may hold values from -150 to 150
- new_keys: bfloat16 [256, 6, 1024], P('dp', None, 'tensor'), may hold values from -6 to 6
- new_values: bfloat16 [256, 6, 1024], P('dp', None, 'tensor'), may hold values from -6 to 6
- key_cache: bfloat16 [256, 256, 1024], P('dp', None, 'tensor'), may hold values from -6 to 6
- value_cache: bfloat16 [256, 256, 1024], P('dp', None, 'tensor'), may hold values from -6 to 6
- cache_lengths: int32 [256], P('dp'), may hold values from 32 to 256, as said below
- accepted: int32 [256], P('tensor'), may hold values from 1 to 6
- residual: bfloat16 [256, 6, 8192], P('tensor', None, 'dp'), may hold values from -6 to 6
- out_weight: bfloat16 [8192, 8192], P('tensor', 'dp'), may hold values from -0.0625 to 0.0625
- draft_weight: bfloat16 [8192, 8192], P('tensor', 'dp'), may hold values from -0.0625 to 0.0625
Outputs:
- verified: bfloat16 [256, 6, 8192], P('tensor', None, 'dp')
- drafted: bfloat16 [5, 256, 8192], P(None, 'tensor', 'dp')
Inputs may be any that keep to these rules, and one draw needn't show every extreme that they name: `cache_lengths`: every draw has a window with all 256 slots live.
All inputs are finite; a program needn't handle non-finite values.
Results may differ from a plain program's by a relative error of at most 0.008.
Values may be sent and summed in bfloat16 or wider, within the bound.
No kernel may reach another device: no remote copies, remote signals or barrier semaphores. Data moves between devices by JAX's collectives and lax.ppermute only.
A program may use at most 64 MiB of HBM per device.

v0:
```python
import jax
import jax.numpy as jnp
from jax import lax
from jax.sharding import PartitionSpec as P

HD = 128
STEPS = 5


def widen(drafted_rows):
    wide_rows = lax.all_gather(drafted_rows, "dp", axis=1, tiled=True)
    return lax.all_to_all(wide_rows, "tensor", split_axis=1, concat_axis=0, tiled=True)


def per_device(
    queries,
    new_keys,
    new_values,
    key_cache,
    value_cache,
    cache_lengths,
    accepted,
    residual,
    out_weight,
    draft_weight,
):
    windows_here, tokens_here, query_width = queries.shape
    cache_size = key_cache.shape[1]
    kv_here = new_keys.shape[2] // HD
    group_size = query_width // HD // kv_here
    query_split = queries.reshape(windows_here, tokens_here, kv_here, group_size, HD)
    keys_cached = key_cache.reshape(windows_here, cache_size, kv_here, HD)
    keys_fresh = new_keys.reshape(windows_here, tokens_here, kv_here, HD)
    score_cache = jnp.einsum(
        "wtkgd,wpkd->wkgtp", query_split, keys_cached, preferred_element_type=jnp.float32
    ) * HD ** (-0.5)
    score_fresh = jnp.einsum(
        "wtkgd,wpkd->wkgtp", query_split, keys_fresh, preferred_element_type=jnp.float32
    ) * HD ** (-0.5)
    live_cache = (jnp.arange(cache_size)[None, :] < cache_lengths[:, None])[:, None, None, None, :]
    live_fresh = jnp.arange(tokens_here)[None, :] <= jnp.arange(tokens_here)[:, None]
    scores = jnp.concatenate(
        [
            jnp.where(live_cache, score_cache, -jnp.inf),
            jnp.where(live_fresh, score_fresh, -jnp.inf),
        ],
        axis=-1,
    )
    largest = jnp.max(scores, axis=-1, keepdims=True)
    powered = jnp.exp(scores - largest)
    weights = (powered / jnp.sum(powered, axis=-1, keepdims=True)).astype(jnp.bfloat16)
    values_cached = value_cache.reshape(windows_here, cache_size, kv_here, HD)
    values_fresh = new_values.reshape(windows_here, tokens_here, kv_here, HD)
    mixed_rows = jnp.einsum(
        "wkgtp,wpkd->wtkgd",
        weights[..., :cache_size],
        values_cached,
        preferred_element_type=jnp.float32,
    )
    mixed_rows = mixed_rows + jnp.einsum(
        "wkgtp,wpkd->wtkgd",
        weights[..., cache_size:],
        values_fresh,
        preferred_element_type=jnp.float32,
    )
    attended = mixed_rows.astype(jnp.bfloat16).reshape(windows_here * tokens_here, query_width)
    partial_out = jnp.dot(
        lax.all_gather(attended, "dp", axis=0, tiled=True),
        out_weight,
        preferred_element_type=jnp.float32,
    )
    summed = lax.psum_scatter(partial_out, "tensor", scatter_dimension=0, tiled=True)
    block_windows, block_tokens, block_cols = residual.shape
    flat_residual = residual.reshape(block_windows * block_tokens, block_cols).astype(jnp.float32)
    verified = (
        (flat_residual + summed)
        .astype(jnp.bfloat16)
        .reshape(block_windows, block_tokens, block_cols)
    )
    chosen = jnp.arange(block_tokens)[None, :] == (accepted - 1)[:, None]
    picked = jnp.sum(
        jnp.where(chosen[:, :, None], verified, jnp.zeros((), jnp.bfloat16)),
        axis=1,
        dtype=jnp.bfloat16,
    )
    results = []
    current = widen(picked)
    row_block = current.shape[0] // lax.axis_size("tensor")
    row_start = lax.axis_index("tensor") * row_block
    for draft_step in range(STEPS):
        everyone = lax.psum(
            jnp.dot(current, draft_weight, preferred_element_type=jnp.float32), "tensor"
        )
        share = lax.dynamic_slice_in_dim(everyone, row_start, row_block, 0)
        drafted_now = jnp.tanh(2.0 * share).astype(jnp.bfloat16)
        results.append(drafted_now)
        if draft_step + 1 < STEPS:
            current = widen(drafted_now)
    return (verified, jnp.stack(results))


def solution(mesh):
    placed = (
        P("dp", None, "tensor"),
        P("dp", None, "tensor"),
        P("dp", None, "tensor"),
        P("dp", None, "tensor"),
        P("dp", None, "tensor"),
        P("dp"),
        P("tensor"),
        P("tensor", None, "dp"),
        P("tensor", "dp"),
        P("tensor", "dp"),
    )
    return jax.shard_map(
        per_device,
        mesh=mesh,
        in_specs=placed,
        out_specs=(P("tensor", None, "dp"), P(None, "tensor", "dp")),
        check_vma=False,
    )
```

profile of v0, /device:TPU:8, one launch (start us, length us, event | category | flops | bytes accessed | tf_op | source)
XLA Modules:
  0.0 744.6 jit_solution(10365520250779408295)
XLA Ops:
  8.1 1.4 fusion.17
  9.5 1.2 fusion.18
  13.0 81.7 %all-gather.2.cloned.1.call-done = bf16[1536,1024]{1,0:T(8,128)(2,1)} async-done(((bf16[48,1024]{1,0:T(8,128)(2,1)}), bf16[1536,1024]{1,0:T(8,128)(2,1)}) %all-gather.2.cloned.1.call-update) | async-done | bytes 3145744 | tf_op jit(solution)/shard_map/all_gather | solution.py:68
  94.7 4.0 fusion.19
  99.0 32.9 %reduce-scatter.2.cloned.1.call-done = f32[192,256]{1,0:T(8,128)} async-done(((f32[1536,256]{1,0:T(8,128)}), f32[192,256]{1,0:T(8,128)}) %reduce-scatter.2.cloned.1.call-update) | async-done | bytes 196624 | tf_op jit(solution)/shard_map/reduce_scatter | solution.py:72
  133.0 43.9 %all_gather.19 = bf16[32,8192]{1,0:T(8,128)(2,1)S(1)} all-gather(bf16[32,256]{1,0:T(8,128)(2,1)S(1)} %select_reduce_fusion), channel_id=1, replica_groups=mesh['dp'=32,'tensor'=8] {'dp'}, dimensions={1}, use_global_device_ids=true | all-gather | bytes 540672 | tf_op jit(solution)/shard_map/all_gather | solution.py:11
  177.0 12.8 %all_to_all.95 = bf16[32,8,1024]{2,0,1:T(8,128)(2,1)S(1)} all-to-all(bf16[32,8,1024]{2,0,1:T(8,128)(2,1)S(1)} %bitcast.106), channel_id=1, replica_groups=mesh['dp'=32,'tensor'=8] {'tensor'}, dimensions={1} | all-to-all | bytes 1048576 | tf_op jit(solution)/shard_map/all_to_all | solution.py:12
  189.8 1.0 fusion.20
  190.9 62.3 %all-reduce.6.cloned.1.call-done = f32[256,256]{1,0:T(8,128)} async-done(((f32[256,256]{1,0:T(8,128)}), f32[256,256]{1,0:T(8,128)}) %all-reduce.6.cloned.1.call-update) | async-done | bytes 262160 | tf_op jit(solution)/shard_map/psum | solution.py:91
  253.9 43.9 %all_gather.20 = bf16[32,8192]{1,0:T(8,128)(2,1)S(1)} all-gather(bf16[32,256]{1,0:T(8,128)(2,1)S(1)} %get-tuple-element.17), channel_id=1, replica_groups=mesh['dp'=32,'tensor'=8] {'dp'}, dimensions={1}, use_global_device_ids=true | all-gather | bytes 540672 | tf_op jit(solution)/shard_map/all_gather | solution.py:11
  297.8 12.8 %all_to_all.96 = bf16[32,8,1024]{2,0,1:T(8,128)(2,1)S(1)} all-to-all(bf16[32,8,1024]{2,0,1:T(8,128)(2,1)S(1)} %bitcast.109), channel_id=1, replica_groups=mesh['dp'=32,'tensor'=8] {'tensor'}, dimensions={1} | all-to-all | bytes 1048576 | tf_op jit(solution)/shard_map/all_to_all | solution.py:12
  310.7 1.0 fusion.21
  311.7 62.2 %all-reduce.8.cloned.1.call-done = f32[256,256]{1,0:T(8,128)} async-done(((f32[256,256]{1,0:T(8,128)}), f32[256,256]{1,0:T(8,128)}) %all-reduce.8.cloned.1.call-update) | async-done | bytes 262160 | tf_op jit(solution)/shard_map/psum | solution.py:91
  374.7 43.9 %all_gather.21 = bf16[32,8192]{1,0:T(8,128)(2,1)S(1)} all-gather(bf16[32,256]{1,0:T(8,128)(2,1)S(1)} %get-tuple-element.15), channel_id=1, replica_groups=mesh['dp'=32,'tensor'=8] {'dp'}, dimensions={1}, use_global_device_ids=true | all-gather | bytes 540672 | tf_op jit(solution)/shard_map/all_gather | solution.py:11
  418.6 12.8 %all_to_all.97 = bf16[32,8,1024]{2,0,1:T(8,128)(2,1)S(1)} all-to-all(bf16[32,8,1024]{2,0,1:T(8,128)(2,1)S(1)} %bitcast.112), channel_id=1, replica_groups=mesh['dp'=32,'tensor'=8] {'tensor'}, dimensions={1} | all-to-all | bytes 1048576 | tf_op jit(solution)/shard_map/all_to_all | solution.py:12
  431.5 1.0 fusion.22
  432.5 62.2 %all-reduce.10.cloned.1.call-done = f32[256,256]{1,0:T(8,128)} async-done(((f32[256,256]{1,0:T(8,128)}), f32[256,256]{1,0:T(8,128)}) %all-reduce.10.cloned.1.call-update) | async-done | bytes 262160 | tf_op jit(solution)/shard_map/psum | solution.py:91
  495.5 43.9 %all_gather.22 = bf16[32,8192]{1,0:T(8,128)(2,1)S(1)} all-gather(bf16[32,256]{1,0:T(8,128)(2,1)S(1)} %get-tuple-element.13), channel_id=1, replica_groups=mesh['dp'=32,'tensor'=8] {'dp'}, dimensions={1}, use_global_device_ids=true | all-gather | bytes 540672 | tf_op jit(solution)/shard_map/all_gather | solution.py:11
  539.5 12.8 %all_to_all.98 = bf16[32,8,1024]{2,0,1:T(8,128)(2,1)S(1)} all-to-all(bf16[32,8,1024]{2,0,1:T(8,128)(2,1)S(1)} %bitcast.115), channel_id=1, replica_groups=mesh['dp'=32,'tensor'=8] {'tensor'}, dimensions={1} | all-to-all | bytes 1048576 | tf_op jit(solution)/shard_map/all_to_all | solution.py:12
  553.3 62.2 %all-reduce.12.cloned.1.call-done = f32[256,256]{1,0:T(8,128)} async-done(((f32[256,256]{1,0:T(8,128)}), f32[256,256]{1,0:T(8,128)}) %all-reduce.12.cloned.1.call-update) | async-done | bytes 262160 | tf_op jit(solution)/shard_map/psum | solution.py:91
  616.3 43.9 %all_gather.23 = bf16[32,8192]{1,0:T(8,128)(2,1)S(1)} all-gather(bf16[32,256]{1,0:T(8,128)(2,1)S(1)} %get-tuple-element.11), channel_id=1, replica_groups=mesh['dp'=32,'tensor'=8] {'dp'}, dimensions={1}, use_global_device_ids=true | all-gather | bytes 540672 | tf_op jit(solution)/shard_map/all_gather | solution.py:11
  660.3 12.8 %all_to_all.99 = bf16[32,8,1024]{2,0,1:T(8,128)(2,1)S(1)} all-to-all(bf16[32,8,1024]{2,0,1:T(8,128)(2,1)S(1)} %bitcast.118), channel_id=1, replica_groups=mesh['dp'=32,'tensor'=8] {'tensor'}, dimensions={1} | all-to-all | bytes 1048576 | tf_op jit(solution)/shard_map/all_to_all | solution.py:12
  673.1 1.0 fusion.24
  674.8 61.6 %all-reduce.14.cloned.1.call-done = f32[256,256]{1,0:T(8,128)} async-done(((f32[256,256]{1,0:T(8,128)}), f32[256,256]{1,0:T(8,128)}) %all-reduce.14.cloned.1.call-update) | async-done | bytes 262160 | tf_op jit(solution)/shard_map/psum | solution.py:91
  (53 shorter events, 11.1 us)
Async XLA Ops:
  7.2 87.5 %copy-start = (bf16[1024,256]{1,0:T(8,128)(2,1)S(1)}, bf16[1024,256]{1,0:T(8,128)(2,1)}, u32[]{:S(2)}) copy-start(bf16[1024,256]{1,0:T(8,128)(2,1)} %param.18) | copy-start | bytes 1572868
  7.2 4.8 copy-start.2
  7.2 87.5 %all-gather.2.cloned.1.call-start = ((), (), s32[]{:S(2)}) async-start(), calls=%async_computation.6 | async-start | bytes 3244032 | tf_op jit(solution)/shard_map/all_gather | solution.py:68
  12.9 85.8 %copy-start.3 = (bf16[32,6,256]{2,0,1:T(8,128)(2,1)S(1)}, bf16[32,6,256]{2,0,1:T(8,128)(2,1)}, u32[]{:S(2)}) copy-start(bf16[32,6,256]{2,0,1:T(8,128)(2,1)} %param.17) | copy-start | bytes 294916
  12.9 86.0 %copy-start.5 = (s32[32]{0:T(128)S(1)}, s32[32]{0:T(128)}, u32[]{:S(2)}) copy-start(s32[32]{0:T(128)} %param.16) | copy-start | bytes 388
  12.9 118.9 %reduce-scatter.2.cloned.1.call-start = ((), (), s32[]{:S(2)}) async-start(), calls=%async_computation.7 | async-start | bytes 1769472 | tf_op jit(solution)/shard_map/reduce_scatter | solution.py:72
  98.7 91.1 %copy-start.1 = (bf16[1024,256]{1,0:T(8,128)(2,1)S(1)}, bf16[1024,256]{1,0:T(8,128)(2,1)}, u32[]{:S(2)}) copy-start(bf16[1024,256]{1,0:T(8,128)(2,1)} %param.19) | copy-start | bytes 1572868
  98.7 154.4 %all-reduce.6.cloned.1.call-start = ((), (), s32[]{:S(2)}) async-start(), calls=%async_computation.8 | async-start | bytes 524288 | tf_op jit(solution)/shard_map/psum | solution.py:91
  190.8 183.1 %all-reduce.8.cloned.1.call-start = ((), (), s32[]{:S(2)}) async-start(), calls=%async_computation.9 | async-start | bytes 524288 | tf_op jit(solution)/shard_map/psum | solution.py:91
  311.7 183.1 %all-reduce.10.cloned.1.call-start = ((), (), s32[]{:S(2)}) async-start(), calls=%async_computation.10 | async-start | bytes 524288 | tf_op jit(solution)/shard_map/psum | solution.py:91
  432.5 183.1 %all-reduce.12.cloned.1.call-start = ((), (), s32[]{:S(2)}) async-start(), calls=%async_computation.11 | async-start | bytes 524288 | tf_op jit(solution)/shard_map/psum | solution.py:91
  553.3 183.1 %all-reduce.14.cloned.1.call-start = ((), (), s32[]{:S(2)}) async-start(), calls=%async_computation.12 | async-start | bytes 524288 | tf_op jit(solution)/shard_map/psum | solution.py:91
  737.1 0.6 copy-start.4
Sparse Core Ops, SparseCore 0:
  13.0 81.5 all-gather.1
  98.8 32.9 reduce-scatter.1
  190.9 62.1 all-reduce.5
  311.8 62.0 all-reduce.7
  432.6 62.1 all-reduce.9
  553.4 62.0 all-reduce.11
  674.2 62.1 all-reduce.13
where the time goes:
time: 745 us
  waiting for transfers between devices  425 us (57%)
  blocking collectives  284 us (38%)
  between operations  14.3 us (2%)
  matrix products  12.6 us (2%)
    psum x5, waiting for transfers between devices, per_device(): lax.psum(jnp.dot(current, draft_weight, preferred_element_type=jnp.float3...  311 us
    all_gather x5, blocking collectives, widen(): wide_rows = lax.all_gather(drafted_rows, 'dp', axis=1, tiled=True)  220 us
    all_gather x1, waiting for transfers between devices, per_device(): lax.all_gather(attended, 'dp', axis=0, tiled=True)  81.7 us
    all_to_all x5, blocking collectives, widen(): lax.all_to_all(wide_rows, 'tensor', split_axis=1, concat_axis=0, tiled=True)  64 us
    reduce_scatter x1, waiting for transfers between devices, per_device(): lax.psum_scatter(partial_out, 'tensor', scatter_dimension=0, tiled=True)  32.9 us
  transfers between devices with their start and end apart: 7, of which 7 were waited for; matrix products, arithmetic and copies ran while one was open for 0% of the time, Pallas kernels for 0%

commit v1 on v0

--- a/solution.py
+++ b/solution.py
@@ -88,8 +88,13 @@
     row_block = current.shape[0] // lax.axis_size("tensor")
     row_start = lax.axis_index("tensor") * row_block
     for draft_step in range(STEPS):
-        everyone = lax.psum(
-            jnp.dot(current, draft_weight, preferred_element_type=jnp.float32), "tensor"
+
+        def place_the_steps_all(field, axis_tag):
+            latest = jnp.sum(lax.all_gather(field, axis_tag), 0)
+            return latest
+
+        everyone = place_the_steps_all(
+            jnp.dot(current, draft_weight, preferred_element_type=jnp.float32), axis_tag="tensor"
         )
         share = lax.dynamic_slice_in_dim(everyone, row_start, row_block, 0)
         drafted_now = jnp.tanh(2.0 * share).astype(jnp.bfloat16)

time: 745 us -> 569 us (0.76)
  waiting for transfers between devices: 425 us -> 239 us
    psum x5 -> x0, waiting for transfers between devices: 311 us -> none  [per_device(): lax.psum(jnp.dot(current, draft_weight, preferred_element_type=jnp.float3...]
    all_gather x0 -> x5, waiting for transfers between devices: none -> 124 us  [place_the_steps_all(): latest = jnp.sum(lax.all_gather(field, axis_tag), 0)]
    reduce_sum x0 -> x5, other arithmetic: none -> 8.77 us  [place_the_steps_all(): latest = jnp.sum(lax.all_gather(field, axis_tag), 0)]
where the time goes in v1:
time: 569 us; the launch traced here: 567 us
  blocking collectives  287 us (50%)
  waiting for transfers between devices  239 us (42%)
  between operations  14.4 us (3%)
  matrix products  12 us (2%)
  other arithmetic  11.3 us (2%)
    all_gather x5, blocking collectives, widen(): wide_rows = lax.all_gather(drafted_rows, 'dp', axis=1, tiled=True)  221 us
    all_gather x5, waiting for transfers between devices, place_the_steps_all(): latest = jnp.sum(lax.all_gather(field, axis_tag), 0)  124 us
    all_gather x1, waiting for transfers between devices, per_device(): lax.all_gather(attended, 'dp', axis=0, tiled=True)  81.7 us
    all_to_all x5, blocking collectives, widen(): lax.all_to_all(wide_rows, 'tensor', split_axis=1, concat_axis=0, tiled=True)  66.7 us
    reduce_scatter x1, waiting for transfers between devices, per_device(): lax.psum_scatter(partial_out, 'tensor', scatter_dimension=0, tiled=True)  32.5 us
  transfers between devices with their start and end apart: 7, of which 7 were waited for; matrix products, arithmetic and copies ran while one was open for 0% of the time, Pallas kernels for 0%

profile of v1, /device:TPU:8, one launch (start us, length us, event | category | flops | bytes accessed | tf_op | source)
XLA Modules:
  0.0 566.7 jit_solution(7671966744528057891)
XLA Ops:
  8.1 1.4 fusion.17
  12.3 81.7 %all-gather.12.cloned.1.call-done = bf16[1536,1024]{1,0:T(8,128)(2,1)} async-done(((bf16[48,1024]{1,0:T(8,128)(2,1)}), bf16[1536,1024]{1,0:T(8,128)(2,1)}) %all-gather.12.cloned.1.call-update) | async-done | bytes 3145744 | tf_op jit(solution)/shard_map/all_gather | solution.py:68
  94.0 4.0 fusion.19
  98.7 32.5 %reduce-scatter.2.cloned.1.call-done = f32[192,256]{1,0:T(8,128)} async-done(((f32[1536,256]{1,0:T(8,128)}), f32[192,256]{1,0:T(8,128)}) %reduce-scatter.2.cloned.1.call-update) | async-done | bytes 196624 | tf_op jit(solution)/shard_map/reduce_scatter | solution.py:72
  132.4 43.8 %all_gather.49 = bf16[32,8192]{1,0:T(8,128)(2,1)S(1)} all-gather(bf16[32,256]{1,0:T(8,128)(2,1)S(1)} %select_reduce_fusion), channel_id=1, replica_groups=mesh['dp'=32,'tensor'=8] {'dp'}, dimensions={1}, use_global_device_ids=true | all-gather | bytes 540672 | tf_op jit(solution)/shard_map/all_gather | solution.py:11
  176.3 12.8 %all_to_all.95 = bf16[32,8,1024]{2,0,1:T(8,128)(2,1)S(1)} all-to-all(bf16[32,8,1024]{2,0,1:T(8,128)(2,1)S(1)} %bitcast.116), channel_id=1, replica_groups=mesh['dp'=32,'tensor'=8] {'tensor'}, dimensions={1} | all-to-all | bytes 1048576 | tf_op jit(solution)/shard_map/all_to_all | solution.py:12
  190.2 25.1 %all-gather.14.cloned.1.call-done = f32[2048,256]{1,0:T(8,128)} async-done(((f32[256,256]{1,0:T(8,128)}), f32[2048,256]{1,0:T(8,128)}) %all-gather.14.cloned.1.call-update) | async-done | bytes 2097168 | tf_op jit(solution)/shard_map/all_gather | solution.py:93
  215.3 1.8 reduce_sum.65
  217.1 44.2 %all_gather.52 = bf16[32,8192]{1,0:T(8,128)(2,1)S(1)} all-gather(bf16[32,256]{1,0:T(8,128)(2,1)S(1)} %get-tuple-element.17), channel_id=1, replica_groups=mesh['dp'=32,'tensor'=8] {'dp'}, dimensions={1}, use_global_device_ids=true | all-gather | bytes 540672 | tf_op jit(solution)/shard_map/all_gather | solution.py:11
  261.3 13.5 %all_to_all.96 = bf16[32,8,1024]{2,0,1:T(8,128)(2,1)S(1)} all-to-all(bf16[32,8,1024]{2,0,1:T(8,128)(2,1)S(1)} %bitcast.119), channel_id=1, replica_groups=mesh['dp'=32,'tensor'=8] {'tensor'}, dimensions={1} | all-to-all | bytes 1048576 | tf_op jit(solution)/shard_map/all_to_all | solution.py:12
  275.8 25.0 %all-gather.16.cloned.1.call-done = f32[2048,256]{1,0:T(8,128)} async-done(((f32[256,256]{1,0:T(8,128)}), f32[2048,256]{1,0:T(8,128)}) %all-gather.16.cloned.1.call-update) | async-done | bytes 2097168 | tf_op jit(solution)/shard_map/all_gather | solution.py:93
  300.8 1.8 reduce_sum.66
  302.6 44.2 %all_gather.55 = bf16[32,8192]{1,0:T(8,128)(2,1)S(1)} all-gather(bf16[32,256]{1,0:T(8,128)(2,1)S(1)} %get-tuple-element.15), channel_id=1, replica_groups=mesh['dp'=32,'tensor'=8] {'dp'}, dimensions={1}, use_global_device_ids=true | all-gather | bytes 540672 | tf_op jit(solution)/shard_map/all_gather | solution.py:11
  346.8 13.5 %all_to_all.97 = bf16[32,8,1024]{2,0,1:T(8,128)(2,1)S(1)} all-to-all(bf16[32,8,1024]{2,0,1:T(8,128)(2,1)S(1)} %bitcast.122), channel_id=1, replica_groups=mesh['dp'=32,'tensor'=8] {'tensor'}, dimensions={1} | all-to-all | bytes 1048576 | tf_op jit(solution)/shard_map/all_to_all | solution.py:12
  361.4 25.0 %all-gather.18.cloned.1.call-done = f32[2048,256]{1,0:T(8,128)} async-done(((f32[256,256]{1,0:T(8,128)}), f32[2048,256]{1,0:T(8,128)}) %all-gather.18.cloned.1.call-update) | async-done | bytes 2097168 | tf_op jit(solution)/shard_map/all_gather | solution.py:93
  386.4 1.8 reduce_sum.67
  388.1 44.2 %all_gather.58 = bf16[32,8192]{1,0:T(8,128)(2,1)S(1)} all-gather(bf16[32,256]{1,0:T(8,128)(2,1)S(1)} %get-tuple-element.13), channel_id=1, replica_groups=mesh['dp'=32,'tensor'=8] {'dp'}, dimensions={1}, use_global_device_ids=true | all-gather | bytes 540672 | tf_op jit(solution)/shard_map/all_gather | solution.py:11
  432.4 13.5 %all_to_all.98 = bf16[32,8,1024]{2,0,1:T(8,128)(2,1)S(1)} all-to-all(bf16[32,8,1024]{2,0,1:T(8,128)(2,1)S(1)} %bitcast.125), channel_id=1, replica_groups=mesh['dp'=32,'tensor'=8] {'tensor'}, dimensions={1} | all-to-all | bytes 1048576 | tf_op jit(solution)/shard_map/all_to_all | solution.py:12
  446.9 25.0 %all-gather.20.cloned.1.call-done = f32[2048,256]{1,0:T(8,128)} async-done(((f32[256,256]{1,0:T(8,128)}), f32[2048,256]{1,0:T(8,128)}) %all-gather.20.cloned.1.call-update) | async-done | bytes 2097168 | tf_op jit(solution)/shard_map/all_gather | solution.py:93
  471.9 1.8 reduce_sum.68
  473.7 44.2 %all_gather.61 = bf16[32,8192]{1,0:T(8,128)(2,1)S(1)} all-gather(bf16[32,256]{1,0:T(8,128)(2,1)S(1)} %get-tuple-element.11), channel_id=1, replica_groups=mesh['dp'=32,'tensor'=8] {'dp'}, dimensions={1}, use_global_device_ids=true | all-gather | bytes 540672 | tf_op jit(solution)/shard_map/all_gather | solution.py:11
  517.9 13.5 %all_to_all.99 = bf16[32,8,1024]{2,0,1:T(8,128)(2,1)S(1)} all-to-all(bf16[32,8,1024]{2,0,1:T(8,128)(2,1)S(1)} %bitcast.128), channel_id=1, replica_groups=mesh['dp'=32,'tensor'=8] {'tensor'}, dimensions={1} | all-to-all | bytes 1048576 | tf_op jit(solution)/shard_map/all_to_all | solution.py:12
  533.1 24.4 %all-gather.22.cloned.1.call-done = f32[2048,256]{1,0:T(8,128)} async-done(((f32[256,256]{1,0:T(8,128)}), f32[2048,256]{1,0:T(8,128)}) %all-gather.22.cloned.1.call-update) | async-done | bytes 2097168 | tf_op jit(solution)/shard_map/all_gather | solution.py:93
  557.4 1.8 reduce_sum.69
  (60 shorter events, 12.3 us)
Async XLA Ops:
  7.2 86.8 %copy-start = (bf16[1024,256]{1,0:T(8,128)(2,1)S(1)}, bf16[1024,256]{1,0:T(8,128)(2,1)}, u32[]{:S(2)}) copy-start(bf16[1024,256]{1,0:T(8,128)(2,1)} %param.18) | copy-start | bytes 1572868
  7.2 4.0 copy-start.4
  7.2 4.1 copy-start.2
  7.2 86.8 %all-gather.12.cloned.1.call-start = ((), (), s32[]{:S(2)}) async-start(), calls=%async_computation.6 | async-start | bytes 3244032 | tf_op jit(solution)/shard_map/all_gather | solution.py:68
  12.2 85.9 %copy-start.3 = (bf16[32,6,256]{2,0,1:T(8,128)(2,1)S(1)}, bf16[32,6,256]{2,0,1:T(8,128)(2,1)}, u32[]{:S(2)}) copy-start(bf16[32,6,256]{2,0,1:T(8,128)(2,1)} %param.17) | copy-start | bytes 294916
  12.2 119.0 %reduce-scatter.2.cloned.1.call-start = ((), (), s32[]{:S(2)}) async-start(), calls=%async_computation.7 | async-start | bytes 1769472 | tf_op jit(solution)/shard_map/reduce_scatter | solution.py:72
  98.0 0.7 copy-start.6
  98.0 91.1 %copy-start.1 = (bf16[1024,256]{1,0:T(8,128)(2,1)S(1)}, bf16[1024,256]{1,0:T(8,128)(2,1)}, u32[]{:S(2)}) copy-start(bf16[1024,256]{1,0:T(8,128)(2,1)} %param.19) | copy-start | bytes 1572868
  98.0 117.3 %all-gather.14.cloned.1.call-start = ((), (), s32[]{:S(2)}) async-start(), calls=%async_computation.8 | async-start | bytes 2359296 | tf_op jit(solution)/shard_map/all_gather | solution.py:93
  190.1 110.7 %all-gather.16.cloned.1.call-start = ((), (), s32[]{:S(2)}) async-start(), calls=%async_computation.9 | async-start | bytes 2359296 | tf_op jit(solution)/shard_map/all_gather | solution.py:93
  275.8 110.6 %all-gather.18.cloned.1.call-start = ((), (), s32[]{:S(2)}) async-start(), calls=%async_computation.10 | async-start | bytes 2359296 | tf_op jit(solution)/shard_map/all_gather | solution.py:93
  361.3 110.6 %all-gather.20.cloned.1.call-start = ((), (), s32[]{:S(2)}) async-start(), calls=%async_computation.11 | async-start | bytes 2359296 | tf_op jit(solution)/shard_map/all_gather | solution.py:93
  446.9 110.6 %all-gather.22.cloned.1.call-start = ((), (), s32[]{:S(2)}) async-start(), calls=%async_computation.12 | async-start | bytes 2359296 | tf_op jit(solution)/shard_map/all_gather | solution.py:93
  559.2 0.6 copy-start.5
Sparse Core Ops, SparseCore 0:
  12.3 81.5 all-gather.11
  98.1 33.0 reduce-scatter.1
  190.2 24.9 all-gather.13
  275.9 24.8 all-gather.15
  361.5 24.8 all-gather.17
  447.0 24.8 all-gather.19
  532.5 24.8 all-gather.21
